TPU v7x, 32 devices: a whole 2x2x4 slice. The times are simulated.
32 devices in a mesh: ctx: 8 (over y, x, core), chan: 4 (over z).
Axes of the slice: x: 2, y: 2, z: 4, core: 2. Of those that a mesh axis runs over, the one named last changes fastest.
Arguments:
- features: bfloat16 [3, 8192, 4096], P(None, 'chan', 'ctx'), may hold values from -6 to 6
- short_filter: float32 [3, 3, 8192], P(None, None, 'chan'), may hold values from -3.5 to 3.5
- lengths: int32 [8], P('ctx'), may hold values from 64 to 512, as said below
- offsets: int32 [8], P('ctx'), may hold values from 0 to 8128, as said below
- decay_rates: float32 [16, 1024], P(None, 'chan'), may hold values from 0 to 1, as said below
- residues: float32 [16, 1024], P(None, 'chan'), may hold values from -1 to 1
- skip_weight: float32 [8192], P('chan'), may hold values from -1 to 1
- out_weight: bfloat16 [8192, 4096], P('chan'), may hold values from -0.09375 to 0.09375
Outputs:
- projected: bfloat16 [4096, 4096], P('chan', 'ctx')
Inputs may be any that keep to these rules, and one draw needn't show every extreme that they name: `lengths`: used slots of each shard, counted from slot 0; some shard uses all 512 slots and some only 64. offsets[i] + lengths[i] <= offsets[i + 1]; the first offset is 0. `decay_rates`: positive rates.
All inputs are finite; a program needn't handle non-finite values.
Results may differ from a plain program's by a relative error of at most 0.018.
Values may be sent and summed in bfloat16 or wider, within the bound.
No kernel may reach another device: no remote copies, remote signals or barrier semaphores. Data moves between devices by JAX's collectives and lax.ppermute only.
A program may use at most 192 MiB of HBM per device.

v0:
```python
import jax
import jax.numpy as jnp
from jax import lax
from jax.sharding import PartitionSpec as P

highest = lax.Precision.HIGHEST


def passed_along(array, axis, by):
    length = lax.axis_size(axis)
    pairs = [(i, i + by) for i in range(length) if 0 <= i + by < length]
    return lax.ppermute(array, axis, pairs)


def shortened(array):
    return jax.tree.map(lambda a: a.astype(jnp.bfloat16) if a.dtype == jnp.float32 else a, array)


def block_pass(blocks, firsts, counts, decay_rows, residue):
    groups, per_group, block_count, block_width = blocks.shape
    mode_count = decay_rows.shape[0]
    rate_g = decay_rows.T
    residue_g = residue.T
    lag_index = jnp.arange(block_width)
    lag_float = lag_index.astype(jnp.float32)
    to_end = jnp.exp(-rate_g[:, None, :] * (block_width - 1.0 - lag_float)[None, :, None])
    raw_sums = lax.dot_general(
        blocks.reshape(groups, per_group * block_count, block_width),
        to_end,
        (((2,), (1,)), ((0,), (0,))),
        precision=highest,
    )
    lift = jnp.exp(rate_g[:, None, :] * (block_width - counts.astype(jnp.float32))[None, :, None])
    summary = raw_sums.reshape(groups, per_group, block_count, mode_count) * lift[:, None, :, :]
    difference = (lag_index[:, None] - lag_index[None, :]).astype(jnp.float32)
    distance = jnp.maximum(difference, 0.0)
    toeplitz = jnp.zeros((groups, block_width, block_width), jnp.float32)
    for mode_index in range(mode_count):
        toeplitz = toeplitz + residue_g[:, mode_index, None, None] * jnp.exp(
            -rate_g[:, mode_index, None, None] * distance[None]
        )
    toeplitz = jnp.where((difference >= 0.0)[None], toeplitz, 0.0)
    inner_part = lax.dot_general(blocks, toeplitz, (((3,), (2,)), ((0,), (0,))), precision=highest)
    lasts = firsts + counts.astype(jnp.float32) - 1.0
    gap_matrix = jnp.maximum(firsts[None, :] - lasts[:, None], 0.0)
    earlier_mask = lag_index[:block_count, None] < lag_index[None, :block_count]
    mixing = jnp.where(
        earlier_mask[None, None], jnp.exp(-rate_g[:, :, None, None] * gap_matrix[None, None]), 0.0
    )
    entering = jnp.einsum("gkcm,gmcb->gkbm", summary, mixing, precision=highest)
    return (inner_part, summary, entering, lasts)


def outer_pass(entering, decay_rows, residue, block_width):
    groups, per_group, block_count, mode_count = entering.shape
    rate_g = decay_rows.T
    lag_float = jnp.arange(block_width, dtype=jnp.float32)
    spread_values = residue.T[:, :, None] * jnp.exp(-rate_g[:, :, None] * lag_float[None, None, :])
    outer_part = lax.dot_general(
        entering.reshape(groups, per_group * block_count, mode_count),
        spread_values,
        (((2,), (1,)), ((0,), (0,))),
        precision=highest,
    )
    return outer_part.reshape(groups, per_group, block_count, block_width)


def shards(
    features, short_filter, lengths, offsets, decay_rates, residues, skip_weight, out_weight
):
    kernel_taps = short_filter.shape[1]
    channels = features.shape[1]
    slot_count = features.shape[2]
    groups = decay_rates.shape[1]
    per_group = channels // groups
    block_width = min(128, slot_count)
    length = lengths[0]
    tail_rows = lax.dynamic_slice_in_dim(
        features, length - (kernel_taps - 1), kernel_taps - 1, axis=2
    )
    previous = passed_along(tail_rows, "ctx", 1)
    extended = jnp.concatenate([previous, features], axis=2)
    short_conv = jnp.zeros((3, channels, slot_count), jnp.float32)
    for tap_index in range(kernel_taps):
        window_rows = lax.slice_in_dim(
            extended, kernel_taps - 1 - tap_index, kernel_taps - 1 - tap_index + slot_count, axis=2
        )
        short_conv = short_conv + short_filter[:, tap_index, :, None] * window_rows.astype(
            jnp.float32
        )
    usable = jnp.arange(slot_count) < length
    product = jnp.where(usable, short_conv[1] * short_conv[2], 0.0)
    all_lengths, all_offsets = (
        lax.all_gather(lengths, "ctx", axis=0, tiled=True),
        lax.all_gather(offsets, "ctx", axis=0, tiled=True),
    )
    ctx_count = lax.axis_size("ctx")
    rank_self = lax.axis_index("ctx")
    shared = groups // ctx_count
    decay_mine = lax.dynamic_slice_in_dim(decay_rates, rank_self * shared, shared, 1)
    residue_mine = lax.dynamic_slice_in_dim(residues, rank_self * shared, shared, 1)
    per_shard = slot_count // block_width
    within = jnp.tile(jnp.arange(per_shard) * block_width, ctx_count)
    firsts_all = jnp.repeat(all_offsets, per_shard).astype(jnp.float32) + within.astype(jnp.float32)
    counts_all = jnp.clip(jnp.repeat(all_lengths, per_shard) - within, 0, block_width)
    received = lax.all_to_all(
        product.reshape(groups, per_group, slot_count).astype(jnp.bfloat16),
        "ctx",
        split_axis=0,
        concat_axis=2,
        tiled=True,
    ).astype(jnp.float32)
    item_count = received.shape[1]
    blocks = received.reshape(shared, item_count, ctx_count * per_shard, block_width)
    inner_part, summary, entering, lasts = block_pass(
        blocks, firsts_all, counts_all, decay_mine, residue_mine
    )
    outer_part = outer_pass(entering, decay_mine, residue_mine, block_width)
    result = (inner_part + outer_part).reshape(shared, item_count, ctx_count * slot_count)
    long_conv = lax.all_to_all(
        shortened(result), "ctx", split_axis=2, concat_axis=0, tiled=True
    ).astype(result.dtype)
    long_conv = long_conv.reshape(channels, slot_count)
    mixed_rows = jnp.where(
        usable, short_conv[0] * (long_conv + skip_weight[:, None] * product), 0.0
    ).astype(jnp.bfloat16)
    return lax.psum_scatter(
        lax.dot_general(
            out_weight, mixed_rows, (((0,), (0,)), ((), ())), preferred_element_type=jnp.float32
        ).astype(jnp.bfloat16),
        "chan",
        scatter_dimension=0,
        tiled=True,
    )


def solution(mesh):
    placed = (
        P(None, "chan", "ctx"),
        P(None, None, "chan"),
        P("ctx"),
        P("ctx"),
        P(None, "chan"),
        P(None, "chan"),
        P("chan"),
        P("chan", None),
    )
    return jax.shard_map(
        shards, mesh=mesh, in_specs=placed, out_specs=P("chan", "ctx"), check_vma=False
    )
```

profile of v0, /device:TPU:0, one launch (start us, length us, event | category | flops | bytes accessed | tf_op | source)
XLA Modules:
  0.0 309.9 jit_solution(4460304330251844339)
XLA Ops:
  7.2 2.5 constant_dynamic-slice_fusion
  10.6 2.4 collective-permute-start
  15.8 9.1 %all-reduce.2 = (s32[8]{0:T(128)S(1)}, s32[8]{0:T(128)S(1)}) all-reduce(s32[8]{0:T(128)S(1)} %dynamic-update-slice, s32[8]{0:T(128)S(1)} %dynamic-update-slice.1), channel_id=1, replica_groups=mesh['ctx'=8,'chan'=4] {'ctx'}, use_global_device_ids=true, to_apply=%add | all-reduce | flops 16 | bytes 128
  26.0 12.5 %multiply_add_fusion = f32[3,2048,512]{2,1,0:T(8,128)S(1)} fusion(bf16[3,2048,512]{2,1,0:T(8,128)(2,1)} %param.8, bf16[3,2048,2]{2,1,0:T(8,128)(2,1)S(1)} %copy.38, f32[3,2048]{1,0:T(4,128)S(1)} %get-tuple-element.46, f32[3,2048]{1,0:T(4,128)S(1)} %get-tuple-element.47, f32[3,2048]{1,0:T(4,128)S(1)} %bitcast.143), kind=kLoop, calls=%fused_computation.1 | loop fusion | flops 44040192 | bytes 18972672 | tf_op jit(solution)/shard_map/add | solution.py:88
  38.5 4.5 %copy-done.2 = f32[3,2048,512]{2,1,0:T(8,128)} copy-done((f32[3,2048,512]{2,1,0:T(8,128)}, f32[3,2048,512]{2,1,0:T(8,128)S(1)}, u32[]{:S(2)}) %copy-start.2) | copy-done | bytes 12582936
  43.1 2.5 fusion.11
  45.5 3.7 %all-to-all-start = ((bf16[256,8,512]{2,1,0:T(8,128)(2,1)}), bf16[256,8,512]{2,1,0:T(8,128)(2,1)S(1)}, u32[]{:S(2)}, u32[]{:S(2)}) async-start(bf16[256,8,512]{2,1,0:T(8,128)(2,1)} %fusion.11), calls=%async_computation | async-start | bytes 4194304 | tf_op jit(solution)/shard_map/all_to_all | solution.py:106
  50.3 25.6 %all-to-all-done = bf16[256,8,512]{2,1,0:T(8,128)(2,1)S(1)} async-done(((bf16[256,8,512]{2,1,0:T(8,128)(2,1)}), bf16[256,8,512]{2,1,0:T(8,128)(2,1)S(1)}, u32[]{:S(2)}, u32[]{:S(2)}) %all-to-all-start) | async-done | bytes 2097184 | tf_op jit(solution)/shard_map/all_to_all | solution.py:106
  77.2 3.3 %copy.39 = bf16[32,8,8,512]{3,2,1,0:T(8,128)(2,1)S(1)} copy(bf16[32,8,8,512]{3,1,0,2:T(8,128)(2,1)} %bitcast.141) | data formatting | bytes 4194304 | tf_op jit(solution)/shard_map/all_to_all | solution.py:106
  80.5 2.8 reshape_reshape.3
  83.3 2.6 reshape.334
  85.9 3.4 %fusion.128 = f32[32,256,16]{1,2,0:T(8,128)S(1)} fusion(bf16[32,256,128]{2,1,0:T(8,128)(2,1)} %reshape_reshape.3, f32[128]{0:T(128)S(1)} %convert_subtract_fusion, f32[32,16]{1,0:T(8,128)S(1)} %copy.40), kind=kOutput, calls=%fused_computation.136 | convolution fusion | flops 201392128 | bytes 2624000 | tf_op jit(solution)/shard_map/dot_general | solution.py:27
  89.7 17.6 %fusion.82 = f32[32,8,32,16]{2,1,3,0:T(8,128)} fusion(f32[32,8,32,16]{2,1,3,0:T(8,128)S(1)} %reshape.335, f32[32,32]{1,0:T(8,128)S(1)} %subtract_maximum_fusion, f32[32,16]{1,0:T(8,128)S(1)} %copy.40, pred[32,32]{1,0:T(8,128)(4,1)S(1)} %broadcast_compare_fusion, f32[32,32,16]{1,2,0:T(8,128)S(1)} %multiply_exponential_fusion), kind=kOutput, calls=%fused_computation.93 | convolution fusion | flops 51511296 | bytes 1121280 | tf_op jit(solution)/shard_map/gkcm,gmcb->gkbm/dot_general | solution.py:50
  109.5 7.5 %fusion.123 = f32[32,256,128]{2,1,0:T(8,128)S(1)} fusion(f32[32,256,16]{1,2,0:T(8,128)S(1)} %reshape.336, f32[32,16]{1,0:T(8,128)S(1)} %copy.40, f32[32,16]{1,0:T(8,128)S(1)} %copy.44), kind=kOutput, calls=%fused_computation.130 | convolution fusion | flops 201457664 | bytes 4722688 | tf_op jit(solution)/shard_map/dot_general | solution.py:59
  117.0 9.5 %add_convert_fusion = bf16[32,8,32,128]{3,2,1,0:T(8,128)(2,1)S(1)} fusion(f32[32,8,32,128]{3,2,1,0:T(8,128)S(1)} %bitcast.142, bf16[32,8,32,128]{3,2,1,0:T(8,128)(2,1)S(1)} %copy-done.4, f32[32]{0:T(128)S(1)} %get-tuple-element.29, f32[32]{0:T(128)S(1)} %get-tuple-element.13, f32[32]{0:T(128)S(1)} %get-tuple-element.30, f32[32]{0:T(128)S(1)} %get-tuple-element.14, ...), kind=kOutput, calls=%fused_computation.22 | convolution fusion | flops 1637875712 | bytes 8474624 | tf_op jit(solution)/shard_map/dot_general | solution.py:43
  126.5 6.8 %copy.50 = bf16[32,8,32,128]{0,1,3,2:T(8,128)(2,1)} copy(bf16[32,8,32,128]{3,2,1,0:T(8,128)(2,1)S(1)} %add_convert_fusion) | data formatting | bytes 4194304 | tf_op jit(solution)/shard_map/convert_element_type | solution.py:16
  133.3 10.1 %reshape.351 = bf16[8,2,65536]{2,1,0:T(2,128)(2,1)S(1)} reshape(bf16[4096,8,32]{2,1,0:T(8,128)(2,1)} %bitcast.140) | data formatting | bytes 4194304
  143.5 29.8 %all_to_all.24 = bf16[8,2,65536]{2,1,0:T(2,128)(2,1)} all-to-all(bf16[8,2,65536]{2,1,0:T(2,128)(2,1)S(1)} %reshape.351), channel_id=1, replica_groups=mesh['ctx'=8,'chan'=4] {'ctx'}, dimensions={0} | all-to-all | bytes 4194304 | tf_op jit(solution)/shard_map/all_to_all | solution.py:120
  173.2 8.7 %reshape.352 = bf16[4096,8,32]{2,1,0:T(8,128)(2,1)} reshape(bf16[8,2,65536]{2,1,0:T(2,128)(2,1)} %all_to_all.24) | data formatting | bytes 4194304
  181.9 10.2 %convert_bitcast_fusion = f32[8,32,8,512]{1,2,3,0:T(8,128)} fusion(bf16[32,8,8,512]{0,1,3,2:T(8,128)(2,1)} %bitcast.139), kind=kLoop, calls=%fused_computation | loop fusion | flops 1048576 | bytes 6291456 | tf_op jit(solution)/shard_map/convert_element_type | solution.py:122
  192.1 12.0 %copy.47 = f32[8,32,8,512]{3,2,1,0:T(8,128)} copy(f32[8,32,8,512]{1,2,3,0:T(8,128)} %convert_bitcast_fusion) | data formatting | bytes 8388608 | tf_op jit(solution)/shard_map/convert_element_type | solution.py:122
  204.1 6.4 %fusion.8 = bf16[2048,512]{1,0:T(8,128)(2,1)S(1)} fusion(f32[3,2048,512]{2,1,0:T(8,128)} %copy-done.2, f32[8,32,8,512]{3,2,1,0:T(8,128)} %copy.47, f32[2048]{0:T(1024)S(1)} %copy-done.6, pred[512]{0:T(512)(128)(4,1)S(1)} %iota_compare_fusion), kind=kLoop, calls=%fused_computation.16 | loop fusion | flops 7340032 | bytes 18883072 | tf_op jit(solution)/shard_map/convert_element_type | solution.py:126
  210.5 14.0 %fusion.5 = bf16[4096,512]{0,1:T(8,128)(2,1)} fusion(bf16[2048,512]{1,0:T(8,128)(2,1)S(1)} %fusion.8, bf16[2048,4096]{1,0:T(8,128)(2,1)} %param.15), kind=kOutput, calls=%fused_computation.11 | convolution fusion | flops 8592031744 | bytes 23068672 | tf_op jit(solution)/shard_map/dot_general | solution.py:128
  224.5 76.3 %reduce-scatter.2.cloned.1.call-done = bf16[1024,512]{0,1:T(8,128)(2,1)} async-done(((bf16[4096,512]{0,1:T(8,128)(2,1)}), bf16[1024,512]{0,1:T(8,128)(2,1)}) %reduce-scatter.2.cloned.1.call-update) | async-done | bytes 1048592 | tf_op jit(solution)/shard_map/reduce_scatter | solution.py:127
  (56 shorter events, 11.3 us)
Async XLA Ops:
  6.5 42.8 %copy-start = (f32[16,256]{1,0:T(8,128)S(1)}, f32[16,256]{1,0:T(8,128)}, u32[]{:S(2)}) copy-start(f32[16,256]{1,0:T(8,128)} %param.13) | copy-start | bytes 49156
  7.2 6.4 %copy-start.8 = (u32[32]{0:T(128)S(1)}, u32[32]{0:T(128)}, u32[]{:S(2)}) copy-start(u32[32]{0:T(128)} %constant.36) | copy-start | bytes 388
  7.2 17.6 %copy-start.5 = (f32[3,3,2048]{2,1,0:T(4,128)S(1)}, f32[3,3,2048]{2,1,0:T(4,128)}, u32[]{:S(2)}) copy-start(f32[3,3,2048]{2,1,0:T(4,128)} %param.9) | copy-start | bytes 221188
  10.6 14.5 %collective-permute-start = (bf16[3,2048,2]{1,0,2:T(4,128)(2,1)S(1)}, bf16[3,2048,2]{1,0,2:T(4,128)(2,1)S(1)}, u32[]{:S(2)}, u32[]{:S(2)}) collective-permute-start(bf16[3,2048,2]{1,0,2:T(4,128)(2,1)S(1)} %copy.54), channel_id=1, source_target_pairs={{0,4},{4,8},{8,12},{12,16},{16,20},{20,24},{24,28},{1,5},{5,9},{9,... | collective-permute-start | bytes 73736 | tf_op jit(solution)/shard_map/ppermute | solution.py:12
  38.5 4.5 %copy-start.2 = (f32[3,2048,512]{2,1,0:T(8,128)}, f32[3,2048,512]{2,1,0:T(8,128)S(1)}, u32[]{:S(2)}) copy-start(f32[3,2048,512]{2,1,0:T(8,128)S(1)} %multiply_add_fusion) | copy-start | bytes 37748740
  45.5 4.1 %copy-start.7 = (f32[16,256]{1,0:T(8,128)S(1)}, f32[16,256]{1,0:T(8,128)}, u32[]{:S(2)}) copy-start(f32[16,256]{1,0:T(8,128)} %param.12) | copy-start | bytes 49156
  45.5 30.3 %all-to-all-start = ((bf16[256,8,512]{2,1,0:T(8,128)(2,1)}), bf16[256,8,512]{2,1,0:T(8,128)(2,1)S(1)}, u32[]{:S(2)}, u32[]{:S(2)}) async-start(bf16[256,8,512]{2,1,0:T(8,128)(2,1)} %fusion.11), calls=%async_computation | async-start | bytes 4194304 | tf_op jit(solution)/shard_map/all_to_all | solution.py:106
  49.3 251.5 %reduce-scatter.2.cloned.1.call-start = ((), (), s32[]{:S(2)}) async-start(), calls=%async_computation.3 | async-start | bytes 5242880 | tf_op jit(solution)/shard_map/reduce_scatter | solution.py:127
  75.9 1.3 copy-start.3
  109.5 7.5 %copy-start.4 = (bf16[32,8,32,128]{3,2,1,0:T(8,128)(2,1)S(1)}, bf16[32,8,32,128]{3,2,1,0:T(8,128)(2,1)}, u32[]{:S(2)}) copy-start(bf16[32,8,32,128]{3,2,1,0:T(8,128)(2,1)} %reshape.334) | copy-start | bytes 6291460
  192.1 12.0 %copy-start.6 = (f32[2048]{0:T(1024)S(1)}, f32[2048]{0:T(1024)}, u32[]{:S(2)}) copy-start(f32[2048]{0:T(1024)} %param.14) | copy-start | bytes 24580
  224.5 78.6 %copy-start.1 = (f32[16,256]{1,0:T(8,128)S(1)}, f32[16,256]{1,0:T(8,128)}, u32[]{:S(2)}) copy-start(f32[16,256]{1,0:T(8,128)} %param.13) | copy-start | bytes 49156
Sparse Core Ops, SparseCore 0:
  224.6 76.1 reduce-scatter.1
where the time goes:
time: 311 us; the launch traced here: 310 us
  waiting for transfers between devices  102 us (33%)
  local copies, waits for them, and re-layouts  63.9 us (21%)
  matrix products  52 us (17%)
  blocking collectives  38.8 us (12%)
  other arithmetic  32.2 us (10%)
  between operations  15 us (5%)
  starting transfers between devices  6.13 us (2%)
    reduce_scatter x1, waiting for transfers between devices, shards(): lax.psum_scatter(lax.dot_general(out_weight, mixed_rows, (((0,), (0,)), (...  76.3 us
    all_to_all x1, blocking collectives, shards(): lax.all_to_all(shortened(result), 'ctx', split_axis=2, concat_axis=0, til...  29.8 us
    unnamed x28, local copies, waits for them, and re-layouts  27.7 us
    all_to_all x1, waiting for transfers between devices, shards(): lax.all_to_all(product.reshape(groups, per_group, slot_count).astype(jnp....  25.6 us
    dot_general x1, matrix products, block_pass(): entering = jnp.einsum('gkcm,gmcb->gkbm', summary, mixing, precision=highest)  17.6 us
    dot_general x1, matrix products, shards(): lax.dot_general(out_weight, mixed_rows, (((0,), (0,)), ((), ())), preferr...  14 us
    add x1, other arithmetic, shards(): short_conv + short_filter[:, tap_index, :, None] * window_rows.astype(jnp...  12.5 us
    convert_element_type x1, local copies, waits for them, and re-layouts, shards(): long_conv = lax.all_to_all(shortened(result), 'ctx', split_axis=2, concat...  12 us
  transfers between devices with their start and end apart: 3, of which 2 were waited for; matrix products, arithmetic and copies ran while one was open for 1% of the time, Pallas kernels for 0%

commit v1 on v0

--- a/solution.py
+++ b/solution.py
@@ -4,6 +4,29 @@
 from jax.sharding import PartitionSpec as P
 
 highest = lax.Precision.HIGHEST
+
+
+def cut_along(value, dim, size):
+    dims = value.shape
+    blocks = value.reshape(*dims[:dim], size, dims[dim] // size, *dims[dim + 1 :])
+    return jnp.moveaxis(blocks, dim, 0)
+
+
+def joined_along(blocks, dim):
+    blocks = jnp.moveaxis(blocks, 0, dim)
+    dims = blocks.shape
+    return blocks.reshape(*dims[:dim], dims[dim] * dims[dim + 1], *dims[dim + 2 :])
+
+
+def rotated_exchange(shard, axis, split_dim, concat_dim):
+    size, index = (lax.axis_size(axis), lax.axis_index(axis))
+    blocks = cut_along(shard, split_dim, size)
+    outs = [blocks[index]]
+    for hop in range(1, size):
+        sent = blocks[(index + hop) % size]
+        outs.append(lax.ppermute(sent, axis, [(i, (i + hop) % size) for i in range(size)]))
+    blocks = jnp.stack(outs)[(index - jnp.arange(size)) % size]
+    return joined_along(blocks, concat_dim)
 
 
 def passed_along(array, axis, by):
@@ -103,12 +126,8 @@
     within = jnp.tile(jnp.arange(per_shard) * block_width, ctx_count)
     firsts_all = jnp.repeat(all_offsets, per_shard).astype(jnp.float32) + within.astype(jnp.float32)
     counts_all = jnp.clip(jnp.repeat(all_lengths, per_shard) - within, 0, block_width)
-    received = lax.all_to_all(
-        product.reshape(groups, per_group, slot_count).astype(jnp.bfloat16),
-        "ctx",
-        split_axis=0,
-        concat_axis=2,
-        tiled=True,
+    received = rotated_exchange(
+        product.reshape(groups, per_group, slot_count).astype(jnp.bfloat16), "ctx", 0, 2
     ).astype(jnp.float32)
     item_count = received.shape[1]
     blocks = received.reshape(shared, item_count, ctx_count * per_shard, block_width)

time: 311 us -> 315 us (1.013)
  waiting for transfers between devices: 102 us -> 92.4 us
  blocking collectives: 38.8 us -> 43.6 us
  local copies, waits for them, and re-layouts: 63.9 us -> 67.5 us
    all_to_all x1 -> x0, waiting for transfers between devices: 25.6 us -> none  [shards(): lax.all_to_all(product.reshape(groups, per_group, slot_count).astype(jnp....]
    ppermute x0 -> x7, waiting for transfers between devices: none -> 16.2 us  [rotated_exchange(): lax.ppermute(sent, axis, [(i, (i + hop) % size) for i in range(size)])]
    ppermute x0 -> x7, starting transfers between devices: none -> 6.04 us  [rotated_exchange(): lax.ppermute(sent, axis, [(i, (i + hop) % size) for i in range(size)])]
    all_to_all x1, blocking collectives: 29.8 us -> 34.6 us  [shards(): lax.all_to_all(shortened(result), 'ctx', split_axis=2, concat_axis=0, til...]
    all_to_all x1 -> x0, starting transfers between devices: 3.73 us -> none  [shards(): lax.all_to_all(product.reshape(groups, per_group, slot_count).astype(jnp....]
    all_to_all x1 -> x0, local copies, waits for them, and re-layouts: 3.31 us -> none  [shards(): lax.all_to_all(product.reshape(groups, per_group, slot_count).astype(jnp....]
    transpose x0 -> x1, local copies, waits for them, and re-layouts: none -> 3.31 us  [joined_along(): blocks = jnp.moveaxis(blocks, 0, dim)]
    unnamed x28 -> x106, local copies, waits for them, and re-layouts: 27.7 us -> 27.5 us
  transfers between devices with their start and end apart: 3 -> 9, of which waited for: 2 -> 5; matrix products, arithmetic and copies ran while one was open for 1% -> 3% of each run, Pallas kernels for 0% -> 0%
where the time goes in v1:
time: 315 us; the launch traced here: 314 us
  waiting for transfers between devices  92.4 us (29%)
  local copies, waits for them, and re-layouts  67.5 us (21%)
  matrix products  52 us (17%)
  blocking collectives  43.6 us (14%)
  other arithmetic  34.5 us (11%)
  between operations  15.6 us (5%)
  starting transfers between devices  8.4 us (3%)
    reduce_scatter x1, waiting for transfers between devices, shards(): lax.psum_scatter(lax.dot_general(out_weight, mixed_rows, (((0,), (0,)), (...  76.3 us
    all_to_all x1, blocking collectives, shards(): lax.all_to_all(shortened(result), 'ctx', split_axis=2, concat_axis=0, til...  34.6 us
    unnamed x106, local copies, waits for them, and re-layouts  27.5 us
    dot_general x1, matrix products, block_pass(): entering = jnp.einsum('gkcm,gmcb->gkbm', summary, mixing, precision=highest)  17.6 us
    ppermute x7, waiting for transfers between devices, rotated_exchange(): lax.ppermute(sent, axis, [(i, (i + hop) % size) for i in range(size)])  16.2 us
    dot_general x1, matrix products, shards(): lax.dot_general(out_weight, mixed_rows, (((0,), (0,)), ((), ())), preferr...  13.9 us
    add x1, other arithmetic, shards(): short_conv + short_filter[:, tap_index, :, None] * window_rows.astype(jnp...  12.5 us
    convert_element_type x1, local copies, waits for them, and re-layouts, shards(): long_conv = lax.all_to_all(shortened(result), 'ctx', split_axis=2, concat...  12 us
  transfers between devices with their start and end apart: 9, of which 5 were waited for; matrix products, arithmetic and copies ran while one was open for 3% of the time, Pallas kernels for 0%

profile of v1, /device:TPU:0, one launch (start us, length us, event | category | flops | bytes accessed | tf_op | source)
XLA Modules:
  0.0 314.1 jit_solution(4872482775466631838)
XLA Ops:
  7.2 2.5 constant_dynamic-slice_fusion
  10.6 2.4 collective-permute-start
  16.6 9.1 %all-reduce.2 = (s32[8]{0:T(128)S(1)}, s32[8]{0:T(128)S(1)}) all-reduce(s32[8]{0:T(128)S(1)} %dynamic-update-slice, s32[8]{0:T(128)S(1)} %dynamic-update-slice.1), channel_id=1, replica_groups=mesh['ctx'=8,'chan'=4] {'ctx'}, use_global_device_ids=true, to_apply=%add | all-reduce | flops 16 | bytes 128
  29.4 12.5 %multiply_add_fusion = f32[3,2048,512]{2,1,0:T(8,128)S(1)} fusion(bf16[3,2048,512]{2,1,0:T(8,128)(2,1)} %param.8, bf16[3,2048,2]{2,1,0:T(8,128)(2,1)S(1)} %copy.40, f32[3,2048]{1,0:T(4,128)S(1)} %get-tuple-element.54, f32[3,2048]{1,0:T(4,128)S(1)} %get-tuple-element.55, f32[3,2048]{1,0:T(4,128)S(1)} %bitcast.169), kind=kLoop, calls=%fused_computation.2 | loop fusion | flops 44040192 | bytes 18972672 | tf_op jit(solution)/shard_map/add | solution.py:111
  43.0 3.5 %copy-done.2 = f32[3,2048,512]{2,1,0:T(8,128)} copy-done((f32[3,2048,512]{2,1,0:T(8,128)}, f32[3,2048,512]{2,1,0:T(8,128)S(1)}, u32[]{:S(2)}) %copy-start.2) | copy-done | bytes 12582936
  51.1 2.4 collective-permute-start.7
  53.8 2.8 collective-permute-done.1
  61.9 11.1 %collective-permute-done.3 = bf16[32,8,512]{2,1,0:T(8,128)(2,1)S(1)} collective-permute-done((bf16[32,8,512]{2,1,0:T(8,128)(2,1)S(1)}, bf16[32,8,512]{2,1,0:T(8,128)(2,1)S(1)}, u32[]{:S(2)}, u32[]{:S(2)}) %collective-permute-start.3) | collective-permute-done | bytes 262176 | tf_op jit(solution)/shard_map/ppermute | solution.py:27
  75.8 3.3 %copy.41 = bf16[32,8,8,512]{3,2,1,0:T(8,128)(2,1)S(1)} copy(bf16[32,8,8,512]{3,1,0,2:T(8,128)(2,1)} %bitcast.167) | data formatting | bytes 4194304 | tf_op jit(solution)/shard_map/transpose | solution.py:16
  79.1 2.8 reshape_reshape.3
  81.9 2.6 reshape.387
  84.5 3.4 %fusion.127 = f32[32,256,16]{1,2,0:T(8,128)S(1)} fusion(bf16[32,256,128]{2,1,0:T(8,128)(2,1)} %reshape_reshape.3, f32[128]{0:T(128)S(1)} %copy-done.43, f32[32,16]{1,0:T(8,128)S(1)} %copy.42), kind=kOutput, calls=%fused_computation.143 | convolution fusion | flops 201392128 | bytes 2624000 | tf_op jit(solution)/shard_map/dot_general | solution.py:50
  88.4 17.6 %fusion.81 = f32[32,8,32,16]{2,1,3,0:T(8,128)} fusion(f32[32,8,32,16]{2,1,3,0:T(8,128)S(1)} %reshape.388, f32[32,32]{1,0:T(8,128)S(1)} %subtract_maximum_fusion, f32[32,16]{1,0:T(8,128)S(1)} %copy.42, pred[32,32]{1,0:T(8,128)(4,1)S(1)} %copy-done.8, f32[32,32,16]{1,2,0:T(8,128)S(1)} %copy-done.4), kind=kOutput, calls=%fused_computation.93 | convolution fusion | flops 51511296 | bytes 1121280 | tf_op jit(solution)/shard_map/gkcm,gmcb->gkbm/dot_general | solution.py:73
  108.5 7.5 %fusion.122 = f32[32,256,128]{2,1,0:T(8,128)S(1)} fusion(f32[32,256,16]{1,2,0:T(8,128)S(1)} %reshape.389, f32[32,16]{1,0:T(8,128)S(1)} %copy.42, f32[32,16]{1,0:T(8,128)S(1)} %copy.46), kind=kOutput, calls=%fused_computation.137 | convolution fusion | flops 201457664 | bytes 4722688 | tf_op jit(solution)/shard_map/dot_general | solution.py:82
  116.4 9.5 %add_convert_fusion = bf16[32,8,32,128]{3,2,1,0:T(8,128)(2,1)S(1)} fusion(f32[32,8,32,128]{3,2,1,0:T(8,128)S(1)} %bitcast.168, bf16[32,8,32,128]{3,2,1,0:T(8,128)(2,1)S(1)} %copy-done.3, f32[32]{0:T(128)S(1)} %copy-done.12, f32[32]{0:T(128)S(1)} %copy-done.28, f32[32]{0:T(128)S(1)} %copy-done.13, f32[32]{0:T(128)S(1)} %copy-done.29, f32[32]{0:T(128)S(1)} %copy-done.14, ...), kind=kOutput, calls=%fused_computation.21 | convolution fusion | flops 1637875712 | bytes 8474624 | tf_op jit(solution)/shard_map/dot_general | solution.py:66
  125.9 6.8 %copy.52 = bf16[32,8,32,128]{0,1,3,2:T(8,128)(2,1)} copy(bf16[32,8,32,128]{3,2,1,0:T(8,128)(2,1)S(1)} %add_convert_fusion) | data formatting | bytes 4194304 | tf_op jit(solution)/shard_map/convert_element_type | solution.py:39
  132.7 10.1 %reshape.412 = bf16[8,2,65536]{2,1,0:T(2,128)(2,1)S(1)} reshape(bf16[4096,8,32]{2,1,0:T(8,128)(2,1)} %bitcast.165) | data formatting | bytes 4194304
  142.9 34.6 %all_to_all.4 = bf16[8,2,65536]{2,1,0:T(2,128)(2,1)} all-to-all(bf16[8,2,65536]{2,1,0:T(2,128)(2,1)S(1)} %reshape.412), channel_id=1, replica_groups=mesh['ctx'=8,'chan'=4] {'ctx'}, dimensions={0} | all-to-all | bytes 4194304 | tf_op jit(solution)/shard_map/all_to_all | solution.py:139
  177.5 8.7 %reshape.413 = bf16[4096,8,32]{2,1,0:T(8,128)(2,1)} reshape(bf16[8,2,65536]{2,1,0:T(2,128)(2,1)} %all_to_all.4) | data formatting | bytes 4194304
  186.1 10.3 %convert_bitcast_fusion = f32[8,32,8,512]{1,2,3,0:T(8,128)} fusion(bf16[32,8,8,512]{0,1,3,2:T(8,128)(2,1)} %bitcast.164), kind=kLoop, calls=%fused_computation.1 | loop fusion | flops 1048576 | bytes 6291456 | tf_op jit(solution)/shard_map/convert_element_type | solution.py:141
  196.4 12.0 %copy.49 = f32[8,32,8,512]{3,2,1,0:T(8,128)} copy(f32[8,32,8,512]{1,2,3,0:T(8,128)} %convert_bitcast_fusion) | data formatting | bytes 8388608 | tf_op jit(solution)/shard_map/convert_element_type | solution.py:141
  208.4 6.4 %fusion.8 = bf16[2048,512]{1,0:T(8,128)(2,1)S(1)} fusion(f32[3,2048,512]{2,1,0:T(8,128)} %copy-done.2, f32[8,32,8,512]{3,2,1,0:T(8,128)} %copy.49, f32[2048]{0:T(1024)S(1)} %copy-done.6, pred[512]{0:T(512)(128)(4,1)S(1)} %copy-done.10), kind=kLoop, calls=%fused_computation.17 | loop fusion | flops 7340032 | bytes 18883072 | tf_op jit(solution)/shard_map/convert_element_type | solution.py:145
  214.8 13.9 %fusion.5 = bf16[4096,512]{0,1:T(8,128)(2,1)} fusion(bf16[2048,512]{1,0:T(8,128)(2,1)S(1)} %fusion.8, bf16[2048,4096]{1,0:T(8,128)(2,1)} %param.15), kind=kOutput, calls=%fused_computation.12 | convolution fusion | flops 8592031744 | bytes 23068672 | tf_op jit(solution)/shard_map/dot_general | solution.py:147
  228.7 76.3 %reduce-scatter.2.cloned.1.call-done = bf16[1024,512]{0,1:T(8,128)(2,1)} async-done(((bf16[4096,512]{0,1:T(8,128)(2,1)}), bf16[1024,512]{0,1:T(8,128)(2,1)}) %reduce-scatter.2.cloned.1.call-update) | async-done | bytes 1048592 | tf_op jit(solution)/shard_map/reduce_scatter | solution.py:146
  (152 shorter events, 26.5 us)
Async XLA Ops:
  6.5 20.2 %copy-start = (f32[16,256]{1,0:T(8,128)S(1)}, f32[16,256]{1,0:T(8,128)}, u32[]{:S(2)}) copy-start(f32[16,256]{1,0:T(8,128)} %param.13) | copy-start | bytes 49156
  6.5 298.5 %reduce-scatter.2.cloned.1.call-start = ((), (), s32[]{:S(2)}) async-start(), calls=%async_computation.2 | async-start | bytes 5242880 | tf_op jit(solution)/shard_map/reduce_scatter | solution.py:146
  7.2 20.3 %copy-start.5 = (f32[3,3,2048]{2,1,0:T(4,128)S(1)}, f32[3,3,2048]{2,1,0:T(4,128)}, u32[]{:S(2)}) copy-start(f32[3,3,2048]{2,1,0:T(4,128)} %param.9) | copy-start | bytes 221188
  10.6 17.9 %collective-permute-start = (bf16[3,2048,2]{1,0,2:T(4,128)(2,1)S(1)}, bf16[3,2048,2]{1,0,2:T(4,128)(2,1)S(1)}, u32[]{:S(2)}, u32[]{:S(2)}) collective-permute-start(bf16[3,2048,2]{1,0,2:T(4,128)(2,1)S(1)} %copy.56), channel_id=1, source_target_pairs={{0,4},{4,8},{8,12},{12,16},{16,20},{20,24},{24,28},{1,5},{5,9},{9,... | collective-permute-start | bytes 73736 | tf_op jit(solution)/shard_map/ppermute | solution.py:35
  28.4 18.1 %copy-start.9 = (pred[512]{0:T(512)(128)(4,1)}, pred[512]{0:T(512)(128)(4,1)S(1)}, u32[]{:S(2)}) copy-start(pred[512]{0:T(512)(128)(4,1)S(1)} %iota_compare_fusion) | copy-start | bytes 1540
  48.1 8.5 %collective-permute-start.1 = (bf16[32,8,512]{2,1,0:T(8,128)(2,1)}, bf16[32,8,512]{2,1,0:T(8,128)(2,1)}, u32[]{:S(2)}, u32[]{:S(2)}) collective-permute-start(bf16[32,8,512]{2,1,0:T(8,128)(2,1)} %get-tuple-element.15), channel_id=1, source_target_pairs={{0,4},{4,8},{8,12},{12,16},{16,20},{20,24},{24,28},{28,0},{1,5},{5... | collective-permute-start | bytes 786440 | tf_op jit(solution)/shard_map/ppermute | solution.py:27
  48.7 10.6 %collective-permute-start.2 = (bf16[32,8,512]{2,1,0:T(8,128)(2,1)}, bf16[32,8,512]{2,1,0:T(8,128)(2,1)}, u32[]{:S(2)}, u32[]{:S(2)}) collective-permute-start(bf16[32,8,512]{2,1,0:T(8,128)(2,1)} %get-tuple-element.14), channel_id=1, source_target_pairs={{0,8},{4,12},{8,16},{12,20},{16,24},{20,28},{24,0},{28,4},{1,9},{5... | collective-permute-start | bytes 786440 | tf_op jit(solution)/shard_map/ppermute | solution.py:27
  51.1 22.6 %collective-permute-start.7 = (bf16[32,8,512]{2,1,0:T(8,128)(2,1)S(1)}, bf16[32,8,512]{2,1,0:T(8,128)(2,1)S(1)}, u32[]{:S(2)}, u32[]{:S(2)}) collective-permute-start(bf16[32,8,512]{2,1,0:T(8,128)(2,1)S(1)} %get-tuple-element.9), channel_id=1, source_target_pairs={{0,28},{4,0},{8,4},{12,8},{16,12},{20,16},{24,20},{28,24},{1,29},{... | collective-permute-start | bytes 786440 | tf_op jit(solution)/shard_map/ppermute | solution.py:27
  53.4 20.2 %collective-permute-start.6 = (bf16[32,8,512]{2,1,0:T(8,128)(2,1)S(1)}, bf16[32,8,512]{2,1,0:T(8,128)(2,1)S(1)}, u32[]{:S(2)}, u32[]{:S(2)}) collective-permute-start(bf16[32,8,512]{2,1,0:T(8,128)(2,1)S(1)} %get-tuple-element.10), channel_id=1, source_target_pairs={{0,24},{4,28},{8,0},{12,4},{16,8},{20,12},{24,16},{28,20},{1,25},{... | collective-permute-start | bytes 786440 | tf_op jit(solution)/shard_map/ppermute | solution.py:27
  53.8 19.7 %collective-permute-start.5 = (bf16[32,8,512]{2,1,0:T(8,128)(2,1)S(1)}, bf16[32,8,512]{2,1,0:T(8,128)(2,1)S(1)}, u32[]{:S(2)}, u32[]{:S(2)}) collective-permute-start(bf16[32,8,512]{2,1,0:T(8,128)(2,1)S(1)} %get-tuple-element.11), channel_id=1, source_target_pairs={{0,20},{4,24},{8,28},{12,0},{16,4},{20,8},{24,12},{28,16},{1,21},{... | collective-permute-start | bytes 786440 | tf_op jit(solution)/shard_map/ppermute | solution.py:27
  56.7 16.3 %collective-permute-start.3 = (bf16[32,8,512]{2,1,0:T(8,128)(2,1)S(1)}, bf16[32,8,512]{2,1,0:T(8,128)(2,1)S(1)}, u32[]{:S(2)}, u32[]{:S(2)}) collective-permute-start(bf16[32,8,512]{2,1,0:T(8,128)(2,1)S(1)} %get-tuple-element.13), channel_id=1, source_target_pairs={{0,12},{4,16},{8,20},{12,24},{16,28},{20,0},{24,4},{28,8},{1,13},{... | collective-permute-start | bytes 786440 | tf_op jit(solution)/shard_map/ppermute | solution.py:27
  59.3 13.7 %collective-permute-start.4 = (bf16[32,8,512]{2,1,0:T(8,128)(2,1)S(1)}, bf16[32,8,512]{2,1,0:T(8,128)(2,1)S(1)}, u32[]{:S(2)}, u32[]{:S(2)}) collective-permute-start(bf16[32,8,512]{2,1,0:T(8,128)(2,1)S(1)} %get-tuple-element.12), channel_id=1, source_target_pairs={{0,16},{4,20},{8,24},{12,28},{16,0},{20,4},{24,8},{28,12},{1,17},{... | collective-permute-start | bytes 786440 | tf_op jit(solution)/shard_map/ppermute | solution.py:27
  108.2 7.9 %copy-start.3 = (bf16[32,8,32,128]{3,2,1,0:T(8,128)(2,1)S(1)}, bf16[32,8,32,128]{3,2,1,0:T(8,128)(2,1)}, u32[]{:S(2)}) copy-start(bf16[32,8,32,128]{3,2,1,0:T(8,128)(2,1)} %reshape.387) | copy-start | bytes 6291460
  108.2 7.9 %copy-start.11 = (f32[32]{0:T(128)S(1)}, f32[32]{0:T(128)}, u32[]{:S(2)}) copy-start(f32[32]{0:T(128)} %get-tuple-element.36) | copy-start | bytes 388
  108.2 7.9 %copy-start.12 = (f32[32]{0:T(128)S(1)}, f32[32]{0:T(128)}, u32[]{:S(2)}) copy-start(f32[32]{0:T(128)} %get-tuple-element.37) | copy-start | bytes 388
  108.2 7.9 %copy-start.13 = (f32[32]{0:T(128)S(1)}, f32[32]{0:T(128)}, u32[]{:S(2)}) copy-start(f32[32]{0:T(128)} %get-tuple-element.38) | copy-start | bytes 388
  108.2 7.9 %copy-start.14 = (f32[32]{0:T(128)S(1)}, f32[32]{0:T(128)}, u32[]{:S(2)}) copy-start(f32[32]{0:T(128)} %get-tuple-element.39) | copy-start | bytes 388
  108.2 7.9 %copy-start.15 = (f32[32]{0:T(128)S(1)}, f32[32]{0:T(128)}, u32[]{:S(2)}) copy-start(f32[32]{0:T(128)} %get-tuple-element.40) | copy-start | bytes 388
  108.2 7.9 %copy-start.16 = (f32[32]{0:T(128)S(1)}, f32[32]{0:T(128)}, u32[]{:S(2)}) copy-start(f32[32]{0:T(128)} %get-tuple-element.41) | copy-start | bytes 388
  108.3 7.9 %copy-start.17 = (f32[32]{0:T(128)S(1)}, f32[32]{0:T(128)}, u32[]{:S(2)}) copy-start(f32[32]{0:T(128)} %get-tuple-element.42) | copy-start | bytes 388
  108.3 7.9 %copy-start.18 = (f32[32]{0:T(128)S(1)}, f32[32]{0:T(128)}, u32[]{:S(2)}) copy-start(f32[32]{0:T(128)} %get-tuple-element.43) | copy-start | bytes 388
  196.4 12.0 %copy-start.6 = (f32[2048]{0:T(1024)S(1)}, f32[2048]{0:T(1024)}, u32[]{:S(2)}) copy-start(f32[2048]{0:T(1024)} %param.14) | copy-start | bytes 24580
  196.4 12.0 %copy-start.10 = (pred[512]{0:T(512)(128)(4,1)S(1)}, pred[512]{0:T(512)(128)(4,1)}, u32[]{:S(2)}) copy-start(pred[512]{0:T(512)(128)(4,1)} %copy-done.9) | copy-start | bytes 1540
  228.7 78.6 %copy-start.1 = (f32[16,256]{1,0:T(8,128)S(1)}, f32[16,256]{1,0:T(8,128)}, u32[]{:S(2)}) copy-start(f32[16,256]{1,0:T(8,128)} %param.13) | copy-start | bytes 49156
  (30 other events, 217.5 us)
Sparse Core Ops, SparseCore 0:
  228.8 76.1 reduce-scatter.1
